TPU v7x, 512 devices: a whole 4x8x8 slice. The times are simulated.
512 devices in a mesh: row: 16 (over x, z_hi), col: 32 (over z_lo, y, core).
Axes of the slice: x: 4, y: 8, z: 8 (z_hi: 4, z_lo: 2; z = z_hi * 2 + z_lo), core: 2. Of those that a mesh axis runs over, the one named last changes fastest.
Arguments:
- bin_features: bfloat16 [4096, 512], P('row'), may hold values from -6 to 6
- w_left: bfloat16 [512, 32], replicated, may hold values from -0.25 to 0.25
- w_right: bfloat16 [512, 32], replicated, may hold values from -0.25 to 0.25
- depth_kernel: float32 [9, 32], replicated, may hold values from -2 to 2
- w_point: bfloat16 [32, 32], replicated, may hold values from -1 to 1
- w_head: bfloat16 [32, 24], replicated, may hold values from -1 to 1
- cotangent: bfloat16 [24, 4096, 4096], P(None, 'row', 'col'), may hold values from -6 to 6
Outputs:
- grad_features: bfloat16 [4096, 512], P('row')
- grad_w_left: float32 [512, 32], replicated
- grad_w_right: float32 [512, 32], replicated
- grad_kernel: float32 [9, 32], replicated
- grad_point: float32 [32, 32], replicated
- grad_head: float32 [32, 24], replicated
All inputs are finite; a program needn't handle non-finite values.
Results may differ from a plain program's by a relative error of at most 0.019.
Values may be sent and summed in bfloat16 or wider, within the bound.
No kernel may reach another device: no remote copies, remote signals or barrier semaphores. Data moves between devices by JAX's collectives and lax.ppermute only.
A program may use at most 64 MiB of HBM per device.

v0:
```python
import math
import jax
import jax.numpy as jnp
from jax import lax
from jax.sharding import PartitionSpec as P

DILATION_STEP = 4


def from_root(block, axis, source):
    block = jnp.where(lax.axis_index(axis) == source, block, jnp.zeros_like(block))
    return lax.psum(block, axis)


def extended(x, sides, width):
    for axis, dim in sides:
        count, length = (lax.axis_size(axis), x.shape[dim])
        up = [(i, (i + 1) % count) for i in range(count - 1)]
        down = [(j, i) for i, j in up]
        last = lax.slice_in_dim(x, length - width, length, axis=dim)
        first = lax.slice_in_dim(x, 0, width, axis=dim)
        before = lax.ppermute(last, axis, up)
        after = lax.ppermute(first, axis, down)
        x = jnp.concatenate([before, x, after], axis=dim)
    return x


def silu_slope(values):
    logistic = jax.nn.sigmoid(values)
    return logistic * (1.0 + values * (1.0 - logistic))


def depthwise(kernel_taps, padded, output_rows, output_columns):
    result = jnp.zeros((padded.shape[0], output_rows, output_columns), jnp.float32)
    for kernel_tap_row in range(3):
        for kernel_tap_column in range(3):
            result = result + kernel_taps[3 * kernel_tap_row + kernel_tap_column][
                :, None, None
            ] * padded[
                :,
                DILATION_STEP * kernel_tap_row : DILATION_STEP * kernel_tap_row + output_rows,
                DILATION_STEP * kernel_tap_column : DILATION_STEP * kernel_tap_column
                + output_columns,
            ].astype(
                jnp.float32
            )
    return result


def body(bin_features, w_left, w_right, depth_kernel, w_point, w_head, cotangent):
    rows_per_tile = bin_features.shape[0]
    columns_per_tile = cotangent.shape[2]
    chans = w_left.shape[1]
    row_count = lax.axis_size("row")
    col_count = lax.axis_size("col")
    panel_ratio = col_count // row_count
    contact_map_bins = rows_per_tile * row_count
    grad_scale = 1.0 / math.sqrt(contact_map_bins)
    row_index = lax.axis_index("row")
    col_index = lax.axis_index("col")
    left_panel = jnp.dot(bin_features, w_left, preferred_element_type=jnp.float32).astype(
        jnp.bfloat16
    )
    offset = col_index % panel_ratio * columns_per_tile
    own_rows = lax.dynamic_slice_in_dim(bin_features, offset, columns_per_tile, 0)
    right_own = jnp.dot(own_rows, w_right, preferred_element_type=jnp.float32).astype(jnp.bfloat16)
    right_panel = from_root(right_own, "row", col_index // panel_ratio)
    pair_matrix = (
        left_panel.astype(jnp.float32).T[:, :, None] + right_panel.astype(jnp.float32).T[:, None, :]
    ).astype(jnp.bfloat16)
    extended_pair = extended(pair_matrix, (("row", 1), ("col", 2)), DILATION_STEP)
    convolved_map = depthwise(depth_kernel, extended_pair, rows_per_tile, columns_per_tile)
    trunk_gradient = (
        grad_scale
        * jnp.einsum("ch,hij->cij", w_head, cotangent, preferred_element_type=jnp.float32)
    ).astype(jnp.bfloat16)
    grad_hidden = jnp.einsum(
        "co,oij->cij", w_point, trunk_gradient, preferred_element_type=jnp.float32
    )
    convolved_gradient = (grad_hidden * silu_slope(convolved_map)).astype(jnp.bfloat16)
    extended_gradient = extended(convolved_gradient, (("row", 1), ("col", 2)), DILATION_STEP)
    hidden_state = jax.nn.silu(convolved_map).astype(jnp.bfloat16)
    mixed_out = jnp.einsum("co,cij->oij", w_point, hidden_state, preferred_element_type=jnp.float32)
    centre_offset = extended_pair[
        :,
        DILATION_STEP : DILATION_STEP + rows_per_tile,
        DILATION_STEP : DILATION_STEP + columns_per_tile,
    ]
    trunk_matrix = (centre_offset.astype(jnp.float32) + mixed_out).astype(jnp.bfloat16)
    conv_f32 = convolved_gradient.astype(jnp.float32)
    backward_pass = jnp.zeros((chans, rows_per_tile, columns_per_tile), jnp.float32)
    kern_terms = []
    for kernel_tap_row in range(3):
        for kernel_tap_column in range(3):
            backward_pass = backward_pass + depth_kernel[3 * kernel_tap_row + kernel_tap_column][
                :, None, None
            ] * extended_gradient[
                :,
                DILATION_STEP * (2 - kernel_tap_row) : DILATION_STEP * (2 - kernel_tap_row)
                + rows_per_tile,
                DILATION_STEP * (2 - kernel_tap_column) : DILATION_STEP * (2 - kernel_tap_column)
                + columns_per_tile,
            ].astype(
                jnp.float32
            )
            shifted_window = extended_pair[
                :,
                DILATION_STEP * kernel_tap_row : DILATION_STEP * kernel_tap_row + rows_per_tile,
                DILATION_STEP * kernel_tap_column : DILATION_STEP * kernel_tap_column
                + columns_per_tile,
            ].astype(jnp.float32)
            kern_terms.append(jnp.sum(conv_f32 * shifted_window, axis=(1, 2)))
    kernel_part = jnp.stack(kern_terms)
    pair_gradient = trunk_gradient.astype(jnp.float32) + backward_pass
    left_part = jnp.sum(pair_gradient, axis=2).T
    right_part = jnp.sum(pair_gradient, axis=1).T
    point_part = jnp.einsum(
        "fsk,gsk->fg", hidden_state, trunk_gradient, preferred_element_type=jnp.float32
    )
    head_part = jnp.einsum(
        "ydq,gdq->yg", trunk_matrix, cotangent, preferred_element_type=jnp.float32
    )
    grad_left = lax.psum(left_part, "col").astype(jnp.bfloat16)
    column_total = lax.psum(right_part, "row").astype(jnp.bfloat16)
    all_panels = lax.all_gather(column_total, "col", axis=0, tiled=True)
    grad_right = lax.dynamic_slice_in_dim(all_panels, row_index * rows_per_tile, rows_per_tile, 0)
    grad_features = (
        jnp.dot(grad_left, w_left.T, preferred_element_type=jnp.float32)
        + jnp.dot(grad_right, w_right.T, preferred_element_type=jnp.float32)
    ).astype(jnp.bfloat16)
    contract = (((0,), (0,)), ((), ()))
    wleft_part = lax.dot_general(
        bin_features, grad_left, contract, preferred_element_type=jnp.float32
    )
    wright_part = lax.dot_general(
        bin_features, grad_right, contract, preferred_element_type=jnp.float32
    )
    kernel_sum, point_sum, head_sum = lax.psum((kernel_part, point_part, head_part), ("row", "col"))
    wleft_sum, wright_sum = lax.psum((wleft_part, wright_part), "row")
    return (
        grad_features,
        grad_scale * wleft_sum,
        grad_scale * wright_sum,
        grad_scale * kernel_sum,
        grad_scale * point_sum,
        grad_scale * head_sum,
    )


def solution(mesh):
    placed = (P("row", None), P(), P(), P(), P(), P(), P(None, "row", "col"))
    return jax.shard_map(
        body,
        mesh=mesh,
        in_specs=placed,
        out_specs=(P("row", None), P(), P(), P(), P(), P()),
        check_vma=False,
    )
```

profile of v0, /device:TPU:8, one launch (start us, length us, event | category | flops | bytes accessed | tf_op | source)
XLA Modules:
  0.0 674.3 jit_solution(18254187634809960480)
XLA Ops:
  7.3 1.1 fusion.34
  8.4 50.8 %psum.56 = bf16[32,128]{1,0:T(8,128)(2,1)S(1)} all-reduce(bf16[32,128]{1,0:T(8,128)(2,1)S(1)} %fusion.34), channel_id=1, replica_groups=mesh['row'=16,'col'=32] {'row'}, use_global_device_ids=true, to_apply=%region_0.1 | all-reduce | flops 4096 | bytes 16384 | tf_op jit(solution)/shard_map/psum | solution.py:12
  59.2 1.1 fusion.29
  60.5 1.7 add_convert_fusion
  62.2 1.3 collective-permute-start
  63.5 1.3 collective-permute-start.1
  64.8 3.5 multiply_convert_fusion.1
  68.3 1.9 collective-permute-done.1
  70.5 2.9 fusion.51
  73.5 3.6 copy.20
  77.1 3.6 copy.22
  80.8 1.9 collective-permute-start.3
  82.7 2.6 collective-permute-start.2
  85.3 3.3 collective-permute-done.2
  88.6 3.0 copy.21
  91.6 3.0 copy.23
  94.7 7.2 %maximum_maximum_fusion = (bf16[32,264,132]{2,0,1:T(8,128)(2,1)S(1)}, bf16[32,264,132]{2,0,1:T(8,128)(2,1)S(1)}) fusion(bf16[32,4,128]{2,0,1:T(8,128)(2,1)S(1)} %collective-permute-done.1, bf16[32,256,128]{2,0,1:T(8,128)(2,1)} %copy-done.1, bf16[32,4,128]{2,0,1:T(8,128)(2,1)S(1)} %collective-permute-done, bf16[32,264,4]{2,0,1:T(8,128)(2,1)} %copy.21, ...), kind=kLoop, calls=%fused_computation.20 | loop fusion | flops 17842176 | bytes 6758400 | tf_op jit(solution)/shard_map/concatenate | solution.py:24
  101.9 10.2 %multiply_convert_fusion = (bf16[32,256,128]{2,0,1:T(8,128)(2,1)}, f32[32,256,128]{2,0,1:T(8,128)}) fusion(bf16[32,264,132]{2,0,1:T(8,128)(2,1)S(1)} %get-tuple-element.34, f32[32]{0:T(128)S(1)} %get-tuple-element.48, bf16[32,4,128]{2,0,1:T(8,128)(2,1)S(1)} %collective-permute-done.1, bf16[32,256,128]{2,0,1:T(8,128)(2,1)S(1)} %copy-done.2, ...), kind=kLoop, calls=%fused_computation.50 | loop fusion | flops 36700160 | bytes 21087360 | tf_op jit(solution)/shard_map/convert_element_type | solution.py:82
  112.1 3.4 fusion.30
  115.6 3.0 convolution_bitcast_fusion.2
  119.0 13.2 %fusion.23 = (f32[32]{0:T(128)S(1)}, f32[32]{0:T(128)S(1)}, f32[32]{0:T(128)S(1)}, f32[32]{0:T(128)S(1)}, f32[32]{0:T(128)S(1)}, /*index=5*/f32[32]{0:T(128)S(1)...) fusion(bf16[32,264,132]{2,0,1:T(8,128)(2,1)} %copy-done.5, ...), kind=kOutput, calls=%fused_computation.47 | convolution fusion | flops 110100192 | bytes 23186560 | tf_op jit(solution)/shard_map/co,oij->cij/dot_general | solution.py:77
  132.3 96.0 %all-reduce = (f32[9,32]{1,0:T(8,128)S(1)}, f32[32,32]{1,0:T(8,128)S(1)}, f32[32,24]{0,1:T(8,128)S(1)}) all-reduce(f32[9,32]{1,0:T(8,128)S(1)} %stack.39, f32[32,32]{1,0:T(8,128)S(1)} %convolution_bitcast_fusion.2, f32[32,24]{0,1:T(8,128)S(1)} %fusion.30), channel_id=1, replica_groups=mesh['row'=16,'col'=32] {'row','col'}, use_global_device_ids=true, to_apply=%region_16.17 | all-reduce | flops 2080 | bytes 16640 | tf_op jit(solution)/shard_map/psum | solution.py:138
  228.3 0.6 broadcast_multiply_fusion.2
  228.9 0.8 fusion.52
  229.7 2.8 collective-permute-start.4
  232.5 1.5 collective-permute-start.5
  234.0 0.6 broadcast_multiply_fusion.3
  234.6 5.1 collective-permute-done.5
  239.7 1.9 pad_maximum_fusion.3
  241.5 2.9 fusion.50
  244.5 3.6 copy.24
  248.1 3.6 copy.26
  251.8 1.9 collective-permute-start.7
  253.7 3.6 collective-permute-start.6
  257.3 0.6 broadcast_multiply_fusion.4
  257.9 1.6 collective-permute-done.6
  259.5 3.0 copy.25
  262.6 3.0 copy.27
  265.6 7.2 %pad_maximum_fusion.1 = (bf16[32,264,132]{2,0,1:T(8,128)(2,1)S(1)}, bf16[32,264,132]{2,0,1:T(8,128)(2,1)S(1)}) fusion(bf16[32,264,4]{2,0,1:T(8,128)(2,1)} %copy.25, bf16[32,4,128]{2,0,1:T(8,128)(2,1)S(1)} %collective-permute-done.5, bf16[32,256,128]{2,0,1:T(8,128)(2,1)} %get-tuple-element.50, bf16[32,4,128]{2,0,1:T(8,128)(2,1)S(1)} %collective-permute-done.4, ...), kind=kLoop, calls=%fused_computation.22 | loop fusion | flops 17842176 | bytes 6758400 | tf_op jit(solution)/shard_map/concatenate | solution.py:24
  272.9 7.2 %fusion.48 = (f32[32,128]{1,0:T(8,128)S(1)}, f32[32,256]{0,1:T(8,128)S(1)}) fusion(bf16[32,264,132]{2,0,1:T(8,128)(2,1)S(1)} %get-tuple-element.30, f32[32]{0:T(128)S(1)} %get-tuple-element.48, bf16[32,256,128]{2,0,1:T(8,128)(2,1)S(1)} %copy-done.6, bf16[32,4,128]{2,0,1:T(8,128)(2,1)S(1)} %collective-permute-done.4, f32[32]{0:T(128)S(1)} %get-tuple-element.49, ...), kind=kLoop, calls=%fused_computation.100 | loop fusion | flops 33542144 | bytes 16893056 | tf_op jit(solution)/shard_map/reduce_sum | solution.py:116
  280.2 102.3 %psum.57 = bf16[256,32]{1,0:T(8,128)(2,1)S(1)} all-reduce(f32[256,32]{1,0:T(8,128)S(1)} %bitcast.73), channel_id=1, replica_groups=mesh['row'=16,'col'=32] {'col'}, use_global_device_ids=true, to_apply=%region_2.3 | all-reduce | flops 8192 | bytes 49152 | tf_op jit(solution)/shard_map/psum | solution.py:123
  382.4 0.8 convolution_bitcast_fusion.1
  383.5 80.7 %psum.58 = bf16[128,32]{0,1:T(8,128)(2,1)S(1)} all-reduce(f32[128,32]{0,1:T(8,128)S(1)} %bitcast.74), channel_id=1, replica_groups=mesh['row'=16,'col'=32] {'row'}, use_global_device_ids=true, to_apply=%region_4.5 | all-reduce | flops 4096 | bytes 24576 | tf_op jit(solution)/shard_map/psum | solution.py:124
  464.2 35.4 %all_gather.3 = bf16[4096,32]{0,1:T(8,128)(2,1)S(1)} all-gather(bf16[128,32]{0,1:T(8,128)(2,1)S(1)} %psum.58), channel_id=1, replica_groups=mesh['row'=16,'col'=32] {'col'}, dimensions={0}, use_global_device_ids=true | all-gather | bytes 270336 | tf_op jit(solution)/shard_map/all_gather | solution.py:125
  499.6 0.8 convolution_bitcast_fusion
  500.4 1.0 fusion.28
  501.3 164.6 %all-reduce.4.cloned.1.call-done = (f32[512,32]{0,1:T(8,128)}, f32[512,32]{0,1:T(8,128)}) async-done(((f32[512,32]{0,1:T(8,128)}, f32[512,32]{0,1:T(8,128)}), (f32[512,32]{0,1:T(8,128)}, f32[512,32]{0,1:T(8,128)})) %all-reduce.4.cloned.1.call-update) | async-done | bytes 131088 | tf_op jit(solution)/shard_map/psum | solution.py:139
  665.9 1.5 broadcast_multiply_fusion
  (41 shorter events, 1.2 us)
Async XLA Ops:
  7.2 57.7 %copy-start = (bf16[24,256,128]{2,1,0:T(8,128)(2,1)S(1)}, bf16[24,256,128]{2,1,0:T(8,128)(2,1)}, u32[]{:S(2)}) copy-start(bf16[24,256,128]{2,1,0:T(8,128)(2,1)} %param.13) | copy-start | bytes 4718596
  7.2 658.8 %all-reduce.4.cloned.1.call-start = ((), (), s32[]{:S(2)}) async-start(), calls=%async_computation | async-start | bytes 262144 | tf_op jit(solution)/shard_map/psum | solution.py:139
  62.2 8.0 %copy-start.1 = (bf16[32,256,128]{2,0,1:T(8,128)(2,1)}, bf16[32,256,128]{2,0,1:T(8,128)(2,1)S(1)}, u32[]{:S(2)}) copy-start(bf16[32,256,128]{2,0,1:T(8,128)(2,1)S(1)} %add_convert_fusion) | copy-start | bytes 6291460
  62.2 6.1 collective-permute-start
  63.5 6.7 collective-permute-start.1
  73.5 11.8 %copy-start.12 = (f32[9,32]{1,0:T(8,128)S(1)}, f32[9,32]{1,0:T(8,128)}, u32[]{:S(2)}) copy-start(f32[9,32]{1,0:T(8,128)} %param.10) | copy-start | bytes 3460
  80.8 10.9 %collective-permute-start.3 = (bf16[32,264,4]{1,0,2:T(8,128)(2,1)S(1)}, bf16[32,264,4]{1,0,2:T(8,128)(2,1)S(1)}, u32[]{:S(2)}, u32[]{:S(2)}) collective-permute-start(bf16[32,264,4]{1,0,2:T(8,128)(2,1)S(1)} %copy.22), channel_id=1, source_target_pairs={{1,0},{2,1},{3,2},{4,3},{5,4},{6,5},{7,6},{8,7},{9,8},{10,9},{11,1... | collective-permute-start | bytes 202760 | tf_op jit(solution)/shard_map/ppermute | solution.py:23
  82.7 5.9 collective-permute-start.2
  94.7 7.2 %copy-start.2 = (bf16[32,256,128]{2,0,1:T(8,128)(2,1)S(1)}, bf16[32,256,128]{2,0,1:T(8,128)(2,1)}, u32[]{:S(2)}) copy-start(bf16[32,256,128]{2,0,1:T(8,128)(2,1)} %copy-done.1) | copy-start | bytes 6291460
  101.9 10.2 %copy-start.4 = (bf16[32,264,132]{2,0,1:T(8,128)(2,1)}, bf16[32,264,132]{2,0,1:T(8,128)(2,1)S(1)}, u32[]{:S(2)}) copy-start(bf16[32,264,132]{2,0,1:T(8,128)(2,1)S(1)} %get-tuple-element.33) | copy-start | bytes 6690820
  101.9 10.2 %copy-start.5 = (bf16[32,264,132]{2,0,1:T(8,128)(2,1)}, bf16[32,264,132]{2,0,1:T(8,128)(2,1)S(1)}, u32[]{:S(2)}) copy-start(bf16[32,264,132]{2,0,1:T(8,128)(2,1)S(1)} %get-tuple-element.34) | copy-start | bytes 6690820
  101.9 10.2 %copy-start.13 = (bf16[32,32]{1,0:T(8,128)(2,1)S(1)}, bf16[32,32]{1,0:T(8,128)(2,1)}, u32[]{:S(2)}) copy-start(bf16[32,32]{1,0:T(8,128)(2,1)} %param.11) | copy-start | bytes 6148
  115.5 3.1 copy-start.3
  115.5 3.5 copy-start.7
  229.7 4.9 collective-permute-start.4
  232.5 7.2 %collective-permute-start.5 = (bf16[32,4,128]{2,0,1:T(8,128)(2,1)S(1)}, bf16[32,4,128]{2,0,1:T(8,128)(2,1)S(1)}, u32[]{:S(2)}, u32[]{:S(2)}) collective-permute-start(bf16[32,4,128]{2,0,1:T(8,128)(2,1)S(1)} %get-tuple-element.38), channel_id=1, source_target_pairs={{32,0},{64,32},{96,64},{128,96},{160,128},{192,160},{224,192},{256... | collective-permute-start | bytes 98312 | tf_op jit(solution)/shard_map/ppermute | solution.py:23
  251.8 10.8 %collective-permute-start.7 = (bf16[32,264,4]{1,0,2:T(8,128)(2,1)S(1)}, bf16[32,264,4]{1,0,2:T(8,128)(2,1)S(1)}, u32[]{:S(2)}, u32[]{:S(2)}) collective-permute-start(bf16[32,264,4]{1,0,2:T(8,128)(2,1)S(1)} %copy.26), channel_id=1, source_target_pairs={{0,1},{1,2},{2,3},{3,4},{4,5},{5,6},{6,7},{7,8},{8,9},{9,10},{10,1... | collective-permute-start | bytes 202760 | tf_op jit(solution)/shard_map/ppermute | solution.py:22
  253.7 5.8 collective-permute-start.6
  265.6 7.3 %copy-start.6 = (bf16[32,256,128]{2,0,1:T(8,128)(2,1)S(1)}, bf16[32,256,128]{2,0,1:T(8,128)(2,1)}, u32[]{:S(2)}) copy-start(bf16[32,256,128]{2,0,1:T(8,128)(2,1)} %get-tuple-element.50) | copy-start | bytes 6291460
  265.6 7.3 %copy-start.8 = (bf16[32,256,128]{2,0,1:T(8,128)(2,1)S(1)}, bf16[32,256,128]{2,0,1:T(8,128)(2,1)}, u32[]{:S(2)}) copy-start(bf16[32,256,128]{2,0,1:T(8,128)(2,1)} %multiply_convert_fusion.1) | copy-start | bytes 6291460
  272.9 109.6 %copy-start.9 = (bf16[256,512]{1,0:T(8,128)(2,1)S(1)}, bf16[256,512]{1,0:T(8,128)(2,1)}, u32[]{:S(2)}) copy-start(bf16[256,512]{1,0:T(8,128)(2,1)} %param.7) | copy-start | bytes 786436
  272.9 110.4 %copy-start.10 = (bf16[512,32]{0,1:T(8,128)(2,1)S(1)}, bf16[512,32]{0,1:T(8,128)(2,1)}, u32[]{:S(2)}) copy-start(bf16[512,32]{0,1:T(8,128)(2,1)} %param.8) | copy-start | bytes 98308
  272.9 227.5 %copy-start.11 = (bf16[512,32]{0,1:T(8,128)(2,1)S(1)}, bf16[512,32]{0,1:T(8,128)(2,1)}, u32[]{:S(2)}) copy-start(bf16[512,32]{0,1:T(8,128)(2,1)} %param.9) | copy-start | bytes 98308
Sparse Core Ops, SparseCore 0:
  500.5 165.3 all-reduce.3
where the time goes:
time: 675 us; the launch traced here: 674 us
  blocking collectives  365 us (54%)
  waiting for transfers between devices  176 us (26%)
  other arithmetic  39 us (6%)
  local copies, waits for them, and re-layouts  34 us (5%)
  matrix products  28.2 us (4%)
  starting transfers between devices  17 us (3%)
  between operations  14.4 us (2%)
    psum x1, waiting for transfers between devices, body(): wleft_sum, wright_sum = lax.psum((wleft_part, wright_part), 'row')  165 us
    psum x1, blocking collectives, body(): grad_left = lax.psum(left_part, 'col').astype(jnp.bfloat16)  102 us
    psum x1, blocking collectives, body(): lax.psum((kernel_part, point_part, head_part), ('row', 'col'))  96 us
    psum x1, blocking collectives, body(): column_total = lax.psum(right_part, 'row').astype(jnp.bfloat16)  80.7 us
    psum x1, blocking collectives, from_root(): return lax.psum(block, axis)  50.8 us
    all_gather x1, blocking collectives, body(): all_panels = lax.all_gather(column_total, 'col', axis=0, tiled=True)  35.4 us
    concatenate x4, other arithmetic, extended(): x = jnp.concatenate([before, x, after], axis=dim)  16.6 us
  transfers between devices with their start and end apart: 9, of which 5 were waited for; matrix products, arithmetic and copies ran while one was open for 2% of the time, Pallas kernels for 0%

commit v1 on v0

--- a/solution.py
+++ b/solution.py
@@ -5,6 +5,11 @@
 from jax.sharding import PartitionSpec as P
 
 DILATION_STEP = 4
+
+
+def axis_by_axis(value, one, other):
+    inner = lax.psum(value, one)
+    return lax.psum(inner, other)
 
 
 def from_root(block, axis, source):
@@ -135,7 +140,9 @@
     wright_part = lax.dot_general(
         bin_features, grad_right, contract, preferred_element_type=jnp.float32
     )
-    kernel_sum, point_sum, head_sum = lax.psum((kernel_part, point_part, head_part), ("row", "col"))
+    kernel_sum, point_sum, head_sum = axis_by_axis(
+        (kernel_part, point_part, head_part), "row", "col"
+    )
     wleft_sum, wright_sum = lax.psum((wleft_part, wright_part), "row")
     return (
         grad_features,

time: 675 us -> 572 us (0.85)
  blocking collectives: 365 us -> 269 us
    psum x2 -> x1, blocking collectives: 177 us -> 79.6 us  [axis_by_axis(): inner = lax.psum(value, one)]
  transfers between devices with their start and end apart: 9 -> 9, of which waited for: 5 -> 4; matrix products, arithmetic and copies ran while one was open for 2% -> 3% of each run, Pallas kernels for 0% -> 0%
where the time goes in v1:
time: 572 us; the launch traced here: 571 us
  blocking collectives  269 us (47%)
  waiting for transfers between devices  172 us (30%)
  other arithmetic  38.8 us (7%)
  local copies, waits for them, and re-layouts  33.6 us (6%)
  matrix products  25 us (4%)
  starting transfers between devices  18.7 us (3%)
  between operations  14.4 us (3%)
    psum x1, waiting for transfers between devices, body(): wleft_sum, wright_sum = lax.psum((wleft_part, wright_part), 'row')  165 us
    psum x1, blocking collectives, body(): grad_left = lax.psum(left_part, 'col').astype(jnp.bfloat16)  103 us
    psum x1, blocking collectives, axis_by_axis(): inner = lax.psum(value, one)  79.6 us
    psum x1, blocking collectives, from_root(): return lax.psum(block, axis)  50.8 us
    all_gather x1, blocking collectives, body(): all_panels = lax.all_gather(column_total, 'col', axis=0, tiled=True)  35.4 us
    concatenate x4, other arithmetic, extended(): x = jnp.concatenate([before, x, after], axis=dim)  16.8 us
  transfers between devices with their start and end apart: 9, of which 4 were waited for; matrix products, arithmetic and copies ran while one was open for 3% of the time, Pallas kernels for 0%

profile of v1, /device:TPU:8, one launch (start us, length us, event | category | flops | bytes accessed | tf_op | source)
XLA Modules:
  0.0 570.9 jit_solution(9039703027171774402)
XLA Ops:
  7.3 1.1 fusion.34
  8.4 50.8 %psum.77 = bf16[32,128]{1,0:T(8,128)(2,1)S(1)} all-reduce(bf16[32,128]{1,0:T(8,128)(2,1)S(1)} %fusion.34), channel_id=1, replica_groups=mesh['row'=16,'col'=32] {'row'}, use_global_device_ids=true, to_apply=%region_0.1 | all-reduce | flops 4096 | bytes 16384 | tf_op jit(solution)/shard_map/psum | solution.py:17
  59.2 1.1 fusion.29
  60.5 1.7 add_convert_fusion
  62.2 1.3 collective-permute-start
  63.5 1.3 collective-permute-start.1
  64.8 3.5 multiply_convert_fusion.1
  68.3 1.9 collective-permute-done.1
  70.2 0.3 pad_maximum_fusion.2
  70.5 2.9 fusion.51
  73.5 3.6 copy.20
  77.1 3.6 copy.22
  80.8 1.9 collective-permute-start.3
  82.7 2.6 collective-permute-start.2
  85.3 3.3 collective-permute-done.2
  88.6 3.0 copy.21
  91.6 3.0 copy.23
  94.7 7.2 %maximum_maximum_fusion = (bf16[32,264,132]{2,0,1:T(8,128)(2,1)S(1)}, bf16[32,264,132]{2,0,1:T(8,128)(2,1)S(1)}) fusion(bf16[32,4,128]{2,0,1:T(8,128)(2,1)S(1)} %collective-permute-done.1, bf16[32,256,128]{2,0,1:T(8,128)(2,1)} %copy-done.1, bf16[32,4,128]{2,0,1:T(8,128)(2,1)S(1)} %collective-permute-done, bf16[32,264,4]{2,0,1:T(8,128)(2,1)} %copy.21, ...), kind=kLoop, calls=%fused_computation.20 | loop fusion | flops 17842176 | bytes 6758400 | tf_op jit(solution)/shard_map/concatenate | solution.py:29
  101.9 9.8 %multiply_convert_fusion = (bf16[32,256,128]{2,0,1:T(8,128)(2,1)}, f32[32,256,128]{2,0,1:T(8,128)}) fusion(bf16[32,264,132]{2,0,1:T(8,128)(2,1)S(1)} %get-tuple-element.39, f32[32]{0:T(128)S(1)} %get-tuple-element.53, bf16[32,4,128]{2,0,1:T(8,128)(2,1)S(1)} %collective-permute-done.1, bf16[32,256,128]{2,0,1:T(8,128)(2,1)S(1)} %copy-done.2, ...), kind=kLoop, calls=%fused_computation.50 | loop fusion | flops 36700160 | bytes 21087360 | tf_op jit(solution)/shard_map/convert_element_type | solution.py:87
  111.7 10.2 %fusion.23 = (f32[32]{0:T(128)S(1)}, f32[32]{0:T(128)S(1)}, f32[32]{0:T(128)S(1)}, f32[32]{0:T(128)S(1)}, f32[32]{0:T(128)S(1)}, /*index=5*/f32[32]{0:T(128)S(1)...) fusion(bf16[32,264,132]{2,0,1:T(8,128)(2,1)S(1)} %get-tuple-element.39, ...), kind=kOutput, calls=%fused_computation.47 | convolution fusion | flops 110100192 | bytes 23186560 | tf_op jit(solution)/shard_map/co,oij->cij/dot_general | solution.py:82
  121.9 0.8 fusion.52
  122.6 4.5 collective-permute-start.4
  127.2 1.5 collective-permute-start.5
  128.7 3.4 fusion.30
  132.2 1.7 collective-permute-done.5
  133.9 1.9 pad_maximum_fusion.3
  135.8 2.9 fusion.50
  138.7 3.6 copy.24
  142.3 3.6 copy.26
  146.0 1.9 collective-permute-start.7
  147.9 3.6 collective-permute-start.6
  151.6 2.9 convolution_bitcast_fusion.2
  154.5 3.0 copy.25
  157.6 3.0 copy.27
  160.6 7.4 %pad_maximum_fusion.1 = (bf16[32,264,132]{2,0,1:T(8,128)(2,1)S(1)}, bf16[32,264,132]{2,0,1:T(8,128)(2,1)S(1)}) fusion(bf16[32,264,4]{2,0,1:T(8,128)(2,1)} %copy.25, bf16[32,4,128]{2,0,1:T(8,128)(2,1)S(1)} %collective-permute-done.5, bf16[32,256,128]{2,0,1:T(8,128)(2,1)} %get-tuple-element.55, bf16[32,4,128]{2,0,1:T(8,128)(2,1)S(1)} %collective-permute-done.4, ...), kind=kLoop, calls=%fused_computation.22 | loop fusion | flops 17842176 | bytes 6758400 | tf_op jit(solution)/shard_map/concatenate | solution.py:29
  168.1 7.2 %fusion.48 = (f32[32,128]{1,0:T(8,128)S(1)}, f32[32,256]{0,1:T(8,128)S(1)}) fusion(bf16[32,264,132]{2,0,1:T(8,128)(2,1)S(1)} %get-tuple-element.35, f32[32]{0:T(128)S(1)} %get-tuple-element.53, bf16[32,256,128]{2,0,1:T(8,128)(2,1)S(1)} %copy-done.3, bf16[32,4,128]{2,0,1:T(8,128)(2,1)S(1)} %collective-permute-done.4, f32[32]{0:T(128)S(1)} %get-tuple-element.54, ...), kind=kLoop, calls=%fused_computation.100 | loop fusion | flops 33542144 | bytes 16893056 | tf_op jit(solution)/shard_map/reduce_sum | solution.py:121
  175.3 79.6 %all-reduce.1 = (f32[9,32]{1,0:T(8,128)S(1)}, f32[32,32]{1,0:T(8,128)S(1)}, f32[32,24]{0,1:T(8,128)S(1)}, bf16[128,32]{0,1:T(8,128)(2,1)S(1)}) all-reduce(f32[9,32]{1,0:T(8,128)S(1)} %stack.39, f32[32,32]{1,0:T(8,128)S(1)} %convolution_bitcast_fusion.2, f32[32,24]{0,1:T(8,128)S(1)} %fusion.30, ...), channel_id=1, replica_groups=mesh['row'=16,'col'=32] {'row'}, use_global_device_ids=true, to_apply=%region_16.17 | all-reduce | flops 6176 | bytes 41216 | tf_op jit(solution)/shard_map/psum | solution.py:11
  254.9 102.7 %all-reduce = (bf16[256,32]{1,0:T(8,128)(2,1)S(1)}, f32[9,32]{1,0:T(8,128)S(1)}, f32[32,32]{1,0:T(8,128)S(1)}, f32[32,24]{0,1:T(8,128)S(1)}) all-reduce(f32[256,32]{1,0:T(8,128)S(1)} %bitcast.73, f32[9,32]{1,0:T(8,128)S(1)} %get-tuple-element.26, f32[32,32]{1,0:T(8,128)S(1)} %get-tuple-element.27, ...), channel_id=1, replica_groups=mesh['row'=16,'col'=32] {'col'}, use_global_device_ids=true, to_apply=%region_2.3 | all-reduce | flops 10272 | bytes 65792 | tf_op jit(solution)/shard_map/psum | solution.py:128
  357.6 0.8 convolution_bitcast_fusion.1
  358.5 0.2 fusion.54
  358.6 0.6 broadcast_multiply_fusion.3
  359.3 0.6 broadcast_multiply_fusion.2
  359.9 35.4 %all_gather.3 = bf16[4096,32]{0,1:T(8,128)(2,1)S(1)} all-gather(bf16[128,32]{0,1:T(8,128)(2,1)S(1)} %get-tuple-element.29), channel_id=1, replica_groups=mesh['row'=16,'col'=32] {'col'}, dimensions={0}, use_global_device_ids=true | all-gather | bytes 270336 | tf_op jit(solution)/shard_map/all_gather | solution.py:130
  395.3 0.8 convolution_bitcast_fusion
  396.1 1.0 fusion.28
  397.1 0.6 broadcast_multiply_fusion.4
  397.7 164.8 %all-reduce.5.cloned.1.call-done = (f32[512,32]{0,1:T(8,128)}, f32[512,32]{0,1:T(8,128)}) async-done(((f32[512,32]{0,1:T(8,128)}, f32[512,32]{0,1:T(8,128)}), (f32[512,32]{0,1:T(8,128)}, f32[512,32]{0,1:T(8,128)})) %all-reduce.5.cloned.1.call-update) | async-done | bytes 131088 | tf_op jit(solution)/shard_map/psum | solution.py:146
  562.5 1.5 broadcast_multiply_fusion
  (32 shorter events, 0.3 us)
Async XLA Ops:
  7.2 57.7 %copy-start = (bf16[24,256,128]{2,1,0:T(8,128)(2,1)S(1)}, bf16[24,256,128]{2,1,0:T(8,128)(2,1)}, u32[]{:S(2)}) copy-start(bf16[24,256,128]{2,1,0:T(8,128)(2,1)} %param.13) | copy-start | bytes 4718596
  7.2 555.3 %all-reduce.5.cloned.1.call-start = ((), (), s32[]{:S(2)}) async-start(), calls=%async_computation | async-start | bytes 262144 | tf_op jit(solution)/shard_map/psum | solution.py:146
  62.2 8.0 %copy-start.1 = (bf16[32,256,128]{2,0,1:T(8,128)(2,1)}, bf16[32,256,128]{2,0,1:T(8,128)(2,1)S(1)}, u32[]{:S(2)}) copy-start(bf16[32,256,128]{2,0,1:T(8,128)(2,1)S(1)} %add_convert_fusion) | copy-start | bytes 6291460
  62.2 6.1 %collective-permute-start = (bf16[32,4,128]{2,0,1:T(8,128)(2,1)S(1)}, bf16[32,4,128]{2,0,1:T(8,128)(2,1)S(1)}, u32[]{:S(2)}, u32[]{:S(2)}) collective-permute-start(bf16[32,4,128]{2,0,1:T(8,128)(2,1)S(1)} %get-tuple-element.44), channel_id=1, source_target_pairs={{0,32},{32,64},{64,96},{96,128},{128,160},{160,192},{192,224},{224... | collective-permute-start | bytes 98312 | tf_op jit(solution)/shard_map/ppermute | solution.py:27
  63.5 6.7 %collective-permute-start.1 = (bf16[32,4,128]{2,0,1:T(8,128)(2,1)S(1)}, bf16[32,4,128]{2,0,1:T(8,128)(2,1)S(1)}, u32[]{:S(2)}, u32[]{:S(2)}) collective-permute-start(bf16[32,4,128]{2,0,1:T(8,128)(2,1)S(1)} %get-tuple-element.45), channel_id=1, source_target_pairs={{32,0},{64,32},{96,64},{128,96},{160,128},{192,160},{224,192},{256... | collective-permute-start | bytes 98312 | tf_op jit(solution)/shard_map/ppermute | solution.py:28
  73.5 11.8 %copy-start.8 = (f32[9,32]{1,0:T(8,128)S(1)}, f32[9,32]{1,0:T(8,128)}, u32[]{:S(2)}) copy-start(f32[9,32]{1,0:T(8,128)} %param.10) | copy-start | bytes 3460
  80.8 10.9 %collective-permute-start.3 = (bf16[32,264,4]{1,0,2:T(8,128)(2,1)S(1)}, bf16[32,264,4]{1,0,2:T(8,128)(2,1)S(1)}, u32[]{:S(2)}, u32[]{:S(2)}) collective-permute-start(bf16[32,264,4]{1,0,2:T(8,128)(2,1)S(1)} %copy.22), channel_id=1, source_target_pairs={{1,0},{2,1},{3,2},{4,3},{5,4},{6,5},{7,6},{8,7},{9,8},{10,9},{11,1... | collective-permute-start | bytes 202760 | tf_op jit(solution)/shard_map/ppermute | solution.py:28
  82.7 5.9 %collective-permute-start.2 = (bf16[32,264,4]{1,0,2:T(8,128)(2,1)S(1)}, bf16[32,264,4]{1,0,2:T(8,128)(2,1)S(1)}, u32[]{:S(2)}, u32[]{:S(2)}) collective-permute-start(bf16[32,264,4]{1,0,2:T(8,128)(2,1)S(1)} %copy.20), channel_id=1, source_target_pairs={{0,1},{1,2},{2,3},{3,4},{4,5},{5,6},{6,7},{7,8},{8,9},{9,10},{10,1... | collective-permute-start | bytes 202760 | tf_op jit(solution)/shard_map/ppermute | solution.py:27
  94.7 7.2 %copy-start.2 = (bf16[32,256,128]{2,0,1:T(8,128)(2,1)S(1)}, bf16[32,256,128]{2,0,1:T(8,128)(2,1)}, u32[]{:S(2)}) copy-start(bf16[32,256,128]{2,0,1:T(8,128)(2,1)} %copy-done.1) | copy-start | bytes 6291460
  101.9 9.8 %copy-start.9 = (bf16[32,32]{1,0:T(8,128)(2,1)S(1)}, bf16[32,32]{1,0:T(8,128)(2,1)}, u32[]{:S(2)}) copy-start(bf16[32,32]{1,0:T(8,128)(2,1)} %param.11) | copy-start | bytes 6148
  122.6 9.5 %collective-permute-start.4 = (bf16[32,4,128]{2,0,1:T(8,128)(2,1)S(1)}, bf16[32,4,128]{2,0,1:T(8,128)(2,1)S(1)}, u32[]{:S(2)}, u32[]{:S(2)}) collective-permute-start(bf16[32,4,128]{2,0,1:T(8,128)(2,1)S(1)} %get-tuple-element.42), channel_id=1, source_target_pairs={{0,32},{32,64},{64,96},{96,128},{128,160},{160,192},{192,224},{224... | collective-permute-start | bytes 98312 | tf_op jit(solution)/shard_map/ppermute | solution.py:27
  127.2 6.7 %collective-permute-start.5 = (bf16[32,4,128]{2,0,1:T(8,128)(2,1)S(1)}, bf16[32,4,128]{2,0,1:T(8,128)(2,1)S(1)}, u32[]{:S(2)}, u32[]{:S(2)}) collective-permute-start(bf16[32,4,128]{2,0,1:T(8,128)(2,1)S(1)} %get-tuple-element.43), channel_id=1, source_target_pairs={{32,0},{64,32},{96,64},{128,96},{160,128},{192,160},{224,192},{256... | collective-permute-start | bytes 98312 | tf_op jit(solution)/shard_map/ppermute | solution.py:28
  146.0 11.6 %collective-permute-start.7 = (bf16[32,264,4]{1,0,2:T(8,128)(2,1)S(1)}, bf16[32,264,4]{1,0,2:T(8,128)(2,1)S(1)}, u32[]{:S(2)}, u32[]{:S(2)}) collective-permute-start(bf16[32,264,4]{1,0,2:T(8,128)(2,1)S(1)} %copy.26), channel_id=1, source_target_pairs={{0,1},{1,2},{2,3},{3,4},{4,5},{5,6},{6,7},{7,8},{8,9},{9,10},{10,1... | collective-permute-start | bytes 202760 | tf_op jit(solution)/shard_map/ppermute | solution.py:27
  147.9 6.6 %collective-permute-start.6 = (bf16[32,264,4]{1,0,2:T(8,128)(2,1)S(1)}, bf16[32,264,4]{1,0,2:T(8,128)(2,1)S(1)}, u32[]{:S(2)}, u32[]{:S(2)}) collective-permute-start(bf16[32,264,4]{1,0,2:T(8,128)(2,1)S(1)} %copy.24), channel_id=1, source_target_pairs={{1,0},{2,1},{3,2},{4,3},{5,4},{6,5},{7,6},{8,7},{9,8},{10,9},{11,1... | collective-permute-start | bytes 202760 | tf_op jit(solution)/shard_map/ppermute | solution.py:28
  160.6 7.4 %copy-start.3 = (bf16[32,256,128]{2,0,1:T(8,128)(2,1)S(1)}, bf16[32,256,128]{2,0,1:T(8,128)(2,1)}, u32[]{:S(2)}) copy-start(bf16[32,256,128]{2,0,1:T(8,128)(2,1)} %get-tuple-element.55) | copy-start | bytes 6291460
  160.6 7.4 %copy-start.4 = (bf16[32,256,128]{2,0,1:T(8,128)(2,1)S(1)}, bf16[32,256,128]{2,0,1:T(8,128)(2,1)}, u32[]{:S(2)}) copy-start(bf16[32,256,128]{2,0,1:T(8,128)(2,1)} %multiply_convert_fusion.1) | copy-start | bytes 6291460
  168.0 189.6 %copy-start.5 = (bf16[256,512]{1,0:T(8,128)(2,1)S(1)}, bf16[256,512]{1,0:T(8,128)(2,1)}, u32[]{:S(2)}) copy-start(bf16[256,512]{1,0:T(8,128)(2,1)} %param.7) | copy-start | bytes 786436
  168.1 190.4 %copy-start.6 = (bf16[512,32]{0,1:T(8,128)(2,1)S(1)}, bf16[512,32]{0,1:T(8,128)(2,1)}, u32[]{:S(2)}) copy-start(bf16[512,32]{0,1:T(8,128)(2,1)} %param.8) | copy-start | bytes 98308
  168.1 228.0 %copy-start.7 = (bf16[512,32]{0,1:T(8,128)(2,1)S(1)}, bf16[512,32]{0,1:T(8,128)(2,1)}, u32[]{:S(2)}) copy-start(bf16[512,32]{0,1:T(8,128)(2,1)} %param.9) | copy-start | bytes 98308
Sparse Core Ops, SparseCore 0:
  397.2 165.2 all-reduce.4
